TPU v7x, 256 devices: a whole 4x4x8 slice. The times are simulated.
256 devices in a mesh: dom: 8 (over x, core), mem: 32 (over z, y).
Axes of the slice: x: 4, y: 4, z: 8, core: 2. Of those that a mesh axis runs over, the one named last changes fastest.
Arguments:
- background_trajectories: bfloat16 [512, 786432], P('mem', 'dom'), may hold values from -6 to 6
- jittered_measurement: bfloat16 [512, 786432], P('mem', 'dom'), may hold values from -6 to 6
- measurement_inverse_variance: float32 [786432], P('dom'), may hold values from 0.25 to 4
- measured_point_number: int32 [12288], P('dom'), may hold values from 0 to 64
- adjacent_region_list: int32 [12288, 16], P(('dom', 'mem')), may hold values from 0 to 12287, as said below
- nearby_separation_tier: int32 [12288, 16], P(('dom', 'mem')), may hold values from 0 to 7, as said below
Outputs:
- increment: bfloat16 [512, 786432], P('mem', 'dom')
Inputs may be any that keep to these rules, and one draw needn't show every extreme that they name: Cells 0 to measured_point_number[p] - 1 of patch p are the observed ones. `adjacent_region_list`: column 0 of row p is p itself. The other 15 entries are distinct patches (p + o) mod 12288 with 0 < |o| <= 16, and every row holds both o = -16 and o = 16. `nearby_separation_tier`: column 0 is 0; the other columns hold 1 to 7.
All inputs are finite; a program needn't handle non-finite values.
Results may differ from a plain program's by a relative error of at most 0.0059.
Values may be sent and summed in bfloat16 or wider, within the bound.
A program may use at most 128 MiB of HBM per device.

v0:
```python
import math

import jax
import jax.numpy as jnp
from jax import lax
from jax.sharding import PartitionSpec as P

PC = 64
REACH = 16
NCLASS = 8


def with_halo(block, sides, width):
    for axis, dim in sides:
        count = lax.axis_size(axis)
        forward = [(i, i + 1) for i in range(count - 1)]
        forward.append((count - 1, 0))
        backward = [(target, source) for source, target in forward]
        low = lax.ppermute(
            lax.slice_in_dim(block, block.shape[dim] - width, None, axis=dim), axis, forward
        )
        high = lax.ppermute(lax.slice_in_dim(block, 0, width, axis=dim), axis, backward)
        block = jnp.concatenate([low, block, high], axis=dim)
    return block


def gc_taper(taper_cutoff_length):
    return (
        1.0
        - 5.0 / 3.0 * taper_cutoff_length**2
        + 0.625 * taper_cutoff_length**3
        + 0.5 * taper_cutoff_length**4
        - 0.25 * taper_cutoff_length**5
    )


def shards(
    background_trajectories,
    jittered_measurement,
    measurement_inverse_variance,
    measured_point_number,
    adjacent_region_list,
    nearby_separation_tier,
):
    groups = lax.axis_size("mem")
    rim_cells = REACH * PC
    observed = (jnp.arange(PC, dtype=jnp.int32)[None, :] < measured_point_number[:, None]).reshape(
        -1
    )
    measurement_gain_factor = jnp.where(observed, measurement_inverse_variance, jnp.float32(0.0))
    departure_residual = (
        measurement_gain_factor[None, :]
        * (jittered_measurement.astype(jnp.float32) - background_trajectories.astype(jnp.float32))
    ).astype(jnp.bfloat16)
    states, innov_local = (
        lax.all_to_all(background_trajectories, "mem", split_axis=1, concat_axis=0, tiled=True),
        lax.all_to_all(departure_residual, "mem", split_axis=1, concat_axis=0, tiled=True),
    )
    sample_mean_state = jnp.mean(states.astype(jnp.float32), axis=0)
    random_jitter_draws = (states.astype(jnp.float32) - sample_mean_state[None, :]).astype(
        jnp.bfloat16
    )
    padded = with_halo(
        jnp.stack((random_jitter_draws, innov_local)), ((("dom", "mem"), 2),), rim_cells
    )
    disturbed_operator_image = padded[0]
    innov_h = padded[1]
    all_members = disturbed_operator_image.shape[0]
    local_cells = disturbed_operator_image.shape[1] - 2 * rim_cells
    local_patches = local_cells // PC
    all_patches = local_patches * lax.axis_size("dom") * groups
    first_patch = (lax.axis_index("dom") * groups + lax.axis_index("mem")) * local_patches
    own_ids = first_patch + jnp.arange(local_patches, dtype=jnp.int32)[:, None]
    offset = (
        adjacent_region_list - own_ids + all_patches + all_patches // 2
    ) % all_patches - all_patches // 2
    near_local = jnp.arange(local_patches, dtype=jnp.int32)[:, None] + REACH + offset
    taper_weight = gc_taper(nearby_separation_tier.astype(jnp.float32) / NCLASS) / (all_members - 1)
    block_size = math.gcd(local_patches, 8)
    window_patches = block_size + 2 * REACH
    window_slots = jnp.arange(window_patches, dtype=jnp.int32)

    def update_block(counter, increment):
        start_patch = counter * block_size
        own_cols = lax.dynamic_slice_in_dim(
            disturbed_operator_image, (REACH + start_patch) * PC, block_size * PC, 1
        )
        window_cols = lax.dynamic_slice_in_dim(
            disturbed_operator_image, start_patch * PC, window_patches * PC, 1
        )
        window_innov = lax.dynamic_slice_in_dim(innov_h, start_patch * PC, window_patches * PC, 1)
        block_near = lax.dynamic_slice_in_dim(near_local, start_patch, block_size, 0) - start_patch
        block_weights = lax.dynamic_slice_in_dim(taper_weight, start_patch, block_size, 0)
        matches = (block_near[:, :, None] == window_slots[None, None, :]).astype(jnp.float32)
        window_weights = jnp.sum(block_weights[:, :, None] * matches, axis=1)
        covariance = lax.dot_general(
            own_cols, window_cols, (((0,), (0,)), ((), ())), preferred_element_type=jnp.float32
        )
        covariance = (
            covariance.reshape(block_size, PC, window_patches, PC)
            * window_weights[:, None, :, None]
        )
        covariance = covariance.astype(jnp.bfloat16).reshape(block_size * PC, window_patches * PC)
        result_block = lax.dot_general(
            window_innov, covariance, (((1,), (1,)), ((), ())), preferred_element_type=jnp.float32
        )
        return lax.dynamic_update_slice_in_dim(
            increment, result_block.astype(jnp.bfloat16), start_patch * PC, 1
        )

    increment = jnp.zeros((all_members, local_cells), jnp.bfloat16)
    increment = lax.fori_loop(0, local_patches // block_size, update_block, increment)
    return lax.all_to_all(increment, "mem", split_axis=0, concat_axis=1, tiled=True)


def solution(mesh):
    in_specs = (
        P("mem", "dom"),
        P("mem", "dom"),
        P("dom"),
        P("dom"),
        P(("dom", "mem"), None),
        P(("dom", "mem"), None),
    )
    out_specs = P("mem", "dom")
    return jax.shard_map(shards, mesh=mesh, in_specs=in_specs, out_specs=out_specs, check_vma=False)
```

profile of v0, /device:TPU:25, one launch (start us, length us, event | category | flops | bytes accessed | tf_op | source)
XLA Modules:
  0.0 449.8 jit_solution(17350568216986462679)
XLA Ops:
  3.8 11.0 %all-to-all-start = ((bf16[16,32,3072]{2,0,1:T(8,128)(2,1)}), bf16[16,32,3072]{2,0,1:T(8,128)(2,1)S(1)}, u32[]{:S(2)}, u32[]{:S(2)}) async-start(bf16[16,32,3072]{2,0,1:T(8,128)(2,1)} %bitcast.30), calls=%async_computation | async-start | bytes 6291456 | tf_op jit(solution)/shard_map/all_to_all | solution.py:56
  22.2 64.6 %all-to-all-done = bf16[16,32,3072]{2,0,1:T(8,128)(2,1)S(1)} async-done(((bf16[16,32,3072]{2,0,1:T(8,128)(2,1)}), bf16[16,32,3072]{2,0,1:T(8,128)(2,1)S(1)}, u32[]{:S(2)}, u32[]{:S(2)}) %all-to-all-start) | async-done | bytes 3145760 | tf_op jit(solution)/shard_map/all_to_all | solution.py:56
  88.4 6.4 %all-to-all-start.1 = ((bf16[16,32,3072]{2,0,1:T(8,128)(2,1)}), bf16[16,32,3072]{2,0,1:T(8,128)(2,1)S(1)}, u32[]{:S(2)}, u32[]{:S(2)}) async-start(bf16[16,32,3072]{2,0,1:T(8,128)(2,1)} %bitcast.29), calls=%async_computation.1 | async-start | bytes 6291456 | tf_op jit(solution)/shard_map/all_to_all | solution.py:57
  100.0 66.9 %all-to-all-done.1 = bf16[16,32,3072]{2,0,1:T(8,128)(2,1)S(1)} async-done(((bf16[16,32,3072]{2,0,1:T(8,128)(2,1)}), bf16[16,32,3072]{2,0,1:T(8,128)(2,1)S(1)}, u32[]{:S(2)}, u32[]{:S(2)}) %all-to-all-start.1) | async-done | bytes 3145760 | tf_op jit(solution)/shard_map/all_to_all | solution.py:57
  172.8 45.2 %collective-permute-done = bf16[2,512,1024]{2,1,0:T(8,128)(2,1)} collective-permute-done((bf16[2,512,1024]{2,1,0:T(8,128)(2,1)}, bf16[2,512,1024]{2,1,0:T(8,128)(2,1)}, u32[]{:S(2)}, u32[]{:S(2)}) %collective-permute-start) | collective-permute-done | bytes 2097184 | tf_op jit(solution)/shard_map/ppermute | solution.py:19
  218.0 8.1 %pad_maximum_fusion = bf16[2,512,5120]{2,1,0:T(8,128)(2,1)} fusion(bf16[2,512,1024]{2,1,0:T(8,128)(2,1)} %collective-permute-done.1, bf16[1,512,3072]{2,1,0:T(8,128)(2,1)S(1)} %bitcast.28, bf16[1,512,3072]{2,1,0:T(8,128)(2,1)} %fusion.17, bf16[2,512,1024]{2,1,0:T(8,128)(2,1)} %collective-permute-done), kind=kLoop, calls=%fused_computation.13 | loop fusion | flops 41943040 | bytes 20971520 | tf_op jit(solution)/shard_map/concatenate | solution.py:23
  226.1 8.6 %slice_bitcast_fusion = (bf16[512,5120]{1,0:T(8,128)(2,1)}, bf16[512,5120]{1,0:T(8,128)(2,1)}) fusion(bf16[2,512,5120]{2,1,0:T(8,128)(2,1)} %pad_maximum_fusion), kind=kLoop, calls=%fused_computation.17 | loop fusion | bytes 20971520 | tf_op jit(solution)/shard_map/squeeze | solution.py:66
  235.1 130.1 %while.16 = (s32[]{:T(128)}, bf16[512,3072]{1,0:T(8,128)(2,1)S(1)}, bf16[512,5120]{1,0:T(8,128)(2,1)}, bf16[512,5120]{1,0:T(8,128)(2,1)}, s32[48,16]{1,0:T(8,128...) while((s32[]{:T(128)}, bf16[512,3072]{1,0:T(8,128)(2,1)S(1)}, ...), condition=%wide.region_3.4_spmd.clone, body=%wide.region_1.3_spmd.clone.sunk | while | flops 2687253248 | bytes 27270984 | solution.py:112
  235.2 4.7 %mul.210 = f32[8,64,40,64]{3,2,1,0:T(8,128)} broadcast(f32[8,40]{1,0:T(8,128)S(1)} %select_reduce_fusion.2), dimensions={0,2} | broadcast | bytes 5244160 | tf_op jit(solution)/shard_map/while/body/eval_jaxpr/mul | solution.py:100
  240.0 9.7 %mul.211 = f32[512,2560]{1,0:T(8,128)} reshape(f32[8,64,40,64]{3,2,1,0:T(8,128)} %mul.210) | data formatting | bytes 10485760 | tf_op jit(solution)/shard_map/while/body/eval_jaxpr/mul | solution.py:100
  249.6 7.1 %fusion.36 = bf16[512,3072]{1,0:T(8,128)(2,1)S(1)} fusion(bf16[512,3072]{1,0:T(8,128)(2,1)S(1)} %get-tuple-element.273, s32[]{:T(128)S(6)} %select_n.69, bf16[512,5120]{1,0:T(8,128)(2,1)} %get-tuple-element.289, s32[]{:T(128)S(6)} %select_n.70, f32[512,2560]{1,0:T(8,128)} %mul.211, bf16[512,5120]{1,0:T(8,128)(2,1)} %get-tuple-element.290, ...), kind=kOutput, calls=%fused_computation.6.clone.1 | convolution fusion | flops 2687238144 | bytes 11536384 | tf_op jit(solution)/shard_map/while/body/eval_jaxpr/dot_general | solution.py:104
  256.9 4.7 %mul.210 = f32[8,64,40,64]{3,2,1,0:T(8,128)} broadcast(f32[8,40]{1,0:T(8,128)S(1)} %select_reduce_fusion.2), dimensions={0,2} | broadcast | bytes 5244160 | tf_op jit(solution)/shard_map/while/body/eval_jaxpr/mul | solution.py:100
  261.7 9.7 %mul.211 = f32[512,2560]{1,0:T(8,128)} reshape(f32[8,64,40,64]{3,2,1,0:T(8,128)} %mul.210) | data formatting | bytes 10485760 | tf_op jit(solution)/shard_map/while/body/eval_jaxpr/mul | solution.py:100
  271.3 7.1 %fusion.36 = bf16[512,3072]{1,0:T(8,128)(2,1)S(1)} fusion(bf16[512,3072]{1,0:T(8,128)(2,1)S(1)} %get-tuple-element.273, s32[]{:T(128)S(6)} %select_n.69, bf16[512,5120]{1,0:T(8,128)(2,1)} %get-tuple-element.289, s32[]{:T(128)S(6)} %select_n.70, f32[512,2560]{1,0:T(8,128)} %mul.211, bf16[512,5120]{1,0:T(8,128)(2,1)} %get-tuple-element.290, ...), kind=kOutput, calls=%fused_computation.6.clone.1 | convolution fusion | flops 2687238144 | bytes 11536384 | tf_op jit(solution)/shard_map/while/body/eval_jaxpr/dot_general | solution.py:104
  278.6 4.7 %mul.210 = f32[8,64,40,64]{3,2,1,0:T(8,128)} broadcast(f32[8,40]{1,0:T(8,128)S(1)} %select_reduce_fusion.2), dimensions={0,2} | broadcast | bytes 5244160 | tf_op jit(solution)/shard_map/while/body/eval_jaxpr/mul | solution.py:100
  283.3 9.7 %mul.211 = f32[512,2560]{1,0:T(8,128)} reshape(f32[8,64,40,64]{3,2,1,0:T(8,128)} %mul.210) | data formatting | bytes 10485760 | tf_op jit(solution)/shard_map/while/body/eval_jaxpr/mul | solution.py:100
  293.0 7.1 %fusion.36 = bf16[512,3072]{1,0:T(8,128)(2,1)S(1)} fusion(bf16[512,3072]{1,0:T(8,128)(2,1)S(1)} %get-tuple-element.273, s32[]{:T(128)S(6)} %select_n.69, bf16[512,5120]{1,0:T(8,128)(2,1)} %get-tuple-element.289, s32[]{:T(128)S(6)} %select_n.70, f32[512,2560]{1,0:T(8,128)} %mul.211, bf16[512,5120]{1,0:T(8,128)(2,1)} %get-tuple-element.290, ...), kind=kOutput, calls=%fused_computation.6.clone.1 | convolution fusion | flops 2687238144 | bytes 11536384 | tf_op jit(solution)/shard_map/while/body/eval_jaxpr/dot_general | solution.py:104
  305.0 9.7 %mul.211 = f32[512,2560]{1,0:T(8,128)} reshape(f32[8,64,40,64]{3,2,1,0:T(8,128)} %mul.210) | data formatting | bytes 10485760 | tf_op jit(solution)/shard_map/while/body/eval_jaxpr/mul | solution.py:100
  314.7 7.1 %fusion.36 = bf16[512,3072]{1,0:T(8,128)(2,1)S(1)} fusion(bf16[512,3072]{1,0:T(8,128)(2,1)S(1)} %get-tuple-element.273, s32[]{:T(128)S(6)} %select_n.69, bf16[512,5120]{1,0:T(8,128)(2,1)} %get-tuple-element.289, s32[]{:T(128)S(6)} %select_n.70, f32[512,2560]{1,0:T(8,128)} %mul.211, bf16[512,5120]{1,0:T(8,128)(2,1)} %get-tuple-element.290, ...), kind=kOutput, calls=%fused_computation.6.clone.1 | convolution fusion | flops 2687238144 | bytes 11536384 | tf_op jit(solution)/shard_map/while/body/eval_jaxpr/dot_general | solution.py:104
  326.7 9.7 %mul.211 = f32[512,2560]{1,0:T(8,128)} reshape(f32[8,64,40,64]{3,2,1,0:T(8,128)} %mul.210) | data formatting | bytes 10485760 | tf_op jit(solution)/shard_map/while/body/eval_jaxpr/mul | solution.py:100
  336.4 7.1 %fusion.36 = bf16[512,3072]{1,0:T(8,128)(2,1)S(1)} fusion(bf16[512,3072]{1,0:T(8,128)(2,1)S(1)} %get-tuple-element.273, s32[]{:T(128)S(6)} %select_n.69, bf16[512,5120]{1,0:T(8,128)(2,1)} %get-tuple-element.289, s32[]{:T(128)S(6)} %select_n.70, f32[512,2560]{1,0:T(8,128)} %mul.211, bf16[512,5120]{1,0:T(8,128)(2,1)} %get-tuple-element.290, ...), kind=kOutput, calls=%fused_computation.6.clone.1 | convolution fusion | flops 2687238144 | bytes 11536384 | tf_op jit(solution)/shard_map/while/body/eval_jaxpr/dot_general | solution.py:104
  348.4 9.7 %mul.211 = f32[512,2560]{1,0:T(8,128)} reshape(f32[8,64,40,64]{3,2,1,0:T(8,128)} %mul.210) | data formatting | bytes 10485760 | tf_op jit(solution)/shard_map/while/body/eval_jaxpr/mul | solution.py:100
  358.1 7.1 %fusion.36 = bf16[512,3072]{1,0:T(8,128)(2,1)S(1)} fusion(bf16[512,3072]{1,0:T(8,128)(2,1)S(1)} %get-tuple-element.273, s32[]{:T(128)S(6)} %select_n.69, bf16[512,5120]{1,0:T(8,128)(2,1)} %get-tuple-element.289, s32[]{:T(128)S(6)} %select_n.70, f32[512,2560]{1,0:T(8,128)} %mul.211, bf16[512,5120]{1,0:T(8,128)(2,1)} %get-tuple-element.290, ...), kind=kOutput, calls=%fused_computation.6.clone.1 | convolution fusion | flops 2687238144 | bytes 11536384 | tf_op jit(solution)/shard_map/while/body/eval_jaxpr/dot_general | solution.py:104
  365.2 82.7 %all_to_all.48 = bf16[32,16,3072]{2,1,0:T(8,128)(2,1)S(1)} all-to-all(bf16[32,16,3072]{2,1,0:T(8,128)(2,1)S(1)} %bitcast.31), channel_id=1, replica_groups=mesh['dom'=8,'mem'=32] {'mem'}, dimensions={0} | all-to-all | bytes 6291456 | tf_op jit(solution)/shard_map/all_to_all | solution.py:113
  (51 shorter events, 41.0 us)
Async XLA Ops:
  3.8 11.1 %copy-start.2 = (s32[1536]{0:T(1024)S(1)}, s32[1536]{0:T(1024)}, u32[]{:S(2)}) copy-start(s32[1536]{0:T(1024)} %param.11) | copy-start | bytes 18436
  3.8 82.9 %all-to-all-start = ((bf16[16,32,3072]{2,0,1:T(8,128)(2,1)}), bf16[16,32,3072]{2,0,1:T(8,128)(2,1)S(1)}, u32[]{:S(2)}, u32[]{:S(2)}) async-start(bf16[16,32,3072]{2,0,1:T(8,128)(2,1)} %bitcast.30), calls=%async_computation | async-start | bytes 6291456 | tf_op jit(solution)/shard_map/all_to_all | solution.py:56
  86.7 1.6 copy-start
  88.4 78.6 %all-to-all-start.1 = ((bf16[16,32,3072]{2,0,1:T(8,128)(2,1)}), bf16[16,32,3072]{2,0,1:T(8,128)(2,1)S(1)}, u32[]{:S(2)}, u32[]{:S(2)}) async-start(bf16[16,32,3072]{2,0,1:T(8,128)(2,1)} %bitcast.29), calls=%async_computation.1 | async-start | bytes 6291456 | tf_op jit(solution)/shard_map/all_to_all | solution.py:57
  94.7 2.8 copy-start.1
  167.0 5.5 %copy-start.4 = (s32[48,16]{0,1:T(8,128)S(1)}, s32[48,16]{0,1:T(8,128)}, u32[]{:S(2)}) copy-start(s32[48,16]{0,1:T(8,128)} %param.12) | copy-start | bytes 9220
  167.0 5.6 %copy-start.3 = (s32[48,16]{0,1:T(8,128)S(1)}, s32[48,16]{0,1:T(8,128)}, u32[]{:S(2)}) copy-start(s32[48,16]{0,1:T(8,128)} %param.13) | copy-start | bytes 9220
  171.0 46.9 %collective-permute-start = (bf16[2,512,1024]{2,1,0:T(8,128)(2,1)}, bf16[2,512,1024]{2,1,0:T(8,128)(2,1)}, u32[]{:S(2)}, u32[]{:S(2)}) collective-permute-start(bf16[2,512,1024]{2,1,0:T(8,128)(2,1)} %get-tuple-element.216), channel_id=1, source_target_pairs={{0,1},{1,2},{2,3},{3,4},{4,5},{5,6},{6,7},{7,8},{8,9},{9,10},{10,1... | collective-permute-start | bytes 6291464 | tf_op jit(solution)/shard_map/ppermute | solution.py:19
  171.0 47.0 %collective-permute-start.1 = (bf16[2,512,1024]{2,1,0:T(8,128)(2,1)}, bf16[2,512,1024]{2,1,0:T(8,128)(2,1)}, u32[]{:S(2)}, u32[]{:S(2)}) collective-permute-start(bf16[2,512,1024]{2,1,0:T(8,128)(2,1)} %get-tuple-element.217), channel_id=1, source_target_pairs={{1,0},{2,1},{3,2},{4,3},{5,4},{6,5},{7,6},{8,7},{9,8},{10,9},{11,1... | collective-permute-start | bytes 6291464 | tf_op jit(solution)/shard_map/ppermute | solution.py:22
where the time goes:
time: 453 us; the launch traced here: 450 us
  waiting for transfers between devices  177 us (39%)
  local copies, waits for them, and re-layouts  105 us (23%)
  blocking collectives  82.7 us (18%)
  matrix products  42.8 us (9%)
  other arithmetic  23.2 us (5%)
  starting transfers between devices  18.9 us (4%)
    mul x12, local copies, waits for them, and re-layouts, update_block(): covariance.reshape(block_size, PC, window_patches, PC)  86.3 us
    all_to_all x1, blocking collectives, shards(): lax.all_to_all(increment, 'mem', split_axis=0, concat_axis=1, tiled=True)  82.7 us
    all_to_all x1, waiting for transfers between devices, shards(): lax.all_to_all(departure_residual, 'mem', split_axis=1, concat_axis=0, ti...  66.9 us
    all_to_all x1, waiting for transfers between devices, shards(): lax.all_to_all(background_trajectories, 'mem', split_axis=1, concat_axis=...  64.6 us
    ppermute x1, waiting for transfers between devices, with_halo(): lax.ppermute(lax.slice_in_dim(block, block.shape[dim] - width, None, axis...  45.2 us
    dot_general x6, matrix products, update_block(): lax.dot_general(window_innov, covariance, (((1,), (1,)), ((), ())), prefe...  42.8 us
    all_to_all x1, starting transfers between devices, shards(): lax.all_to_all(background_trajectories, 'mem', split_axis=1, concat_axis=...  11 us
  transfers between devices with their start and end apart: 4, of which 3 were waited for; matrix products, arithmetic and copies ran while one was open for 3% of the time, Pallas kernels for 0%

commit v1 on v0

v1 whole, which is shorter than its diff:
```python
import jax
import jax.numpy as jnp
from jax import lax
from jax.experimental import pallas as pl
from jax.experimental.pallas import tpu as pltpu
from jax.sharding import PartitionSpec as P

PC = 64
REACH = 16
NCLASS = 8
MEMBERS = 512
GROUPS = 32
SHARE = MEMBERS // GROUPS
OWN = 3072
RIM = REACH * PC
WIDE = OWN + 2 * RIM
BLOCK = 4
ROWS = BLOCK * PC
SPAN = ROWS + 2 * RIM
BLOCKS = OWN // ROWS
PART = OWN // 3


def gc_taper(r):
    return 1.0 - 5.0 / 3.0 * r**2 + 0.625 * r**3 + 0.5 * r**4 - 0.25 * r**5


def mult(value, by):
    return pl.multiple_of(value, by)


def kernel(
    b_ref,
    j_ref,
    g_ref,
    w_ref,
    o_ref,
    bsrc,
    isrc,
    bwin,
    iwin,
    pwin,
    cov,
    obuf,
    wtab,
    wexp,
    lsem,
    wsem,
    bs,
    br,
    bcs,
    bcr,
    js,
    jr,
    jcs,
    jcr,
    hbs,
    hbr,
    hjs,
    hjr,
    osend,
    orecv,
):
    d = lax.axis_index("dom")
    m = lax.axis_index("mem")
    x, c = d // 2, d % 2
    z, y = m // 4, m % 4
    half = m // 16
    place = 2 * (m % 16) + c
    has_left = jnp.logical_or(c == 1, y > 0)
    has_right = jnp.logical_or(c == 0, y < 3)

    def loop(start, stop, body):
        def step(i, carry):
            body(i)
            return carry

        lax.fori_loop(start, stop, step, 0)

    def remote(src, dst, send, recv, dom, mem):
        return pltpu.make_async_remote_copy(
            src_ref=src,
            dst_ref=dst,
            send_sem=send,
            recv_sem=recv,
            device_id={"dom": dom, "mem": mem},
            device_id_type=pl.DeviceIdType.MESH,
        )

    load_b = pltpu.make_async_copy(b_ref, bsrc, lsem.at[0])
    load_j = pltpu.make_async_copy(j_ref, isrc, lsem.at[1])
    load_b.start()
    load_j.start()
    barrier = pltpu.get_barrier_semaphore()

    def greet(t):
        other = (c * 32 + m + t) % 64
        pl.semaphore_signal(
            barrier, inc=1, device_id={"dom": 2 * x + other // 32, "mem": other % 32}
        )

    loop(1, 64, greet)

    @pl.when(jnp.logical_and(c == 0, m == 0))
    def _():
        def greet_lower(t):
            pl.semaphore_signal(
                barrier, inc=1, device_id={"dom": 2 * ((x + 3) % 4) + 1, "mem": t}
            )

        loop(0, GROUPS, greet_lower)

    @pl.when(jnp.logical_and(c == 1, m == GROUPS - 1))
    def _():
        def greet_upper(t):
            pl.semaphore_signal(barrier, inc=1, device_id={"dom": 2 * ((x + 1) % 4), "mem": t})

        loop(0, GROUPS, greet_upper)

    load_b.wait()
    load_j.wait()

    def innovation(k):
        cols = pl.ds(mult(k * OWN, OWN), OWN)
        diff = isrc[:, cols].astype(jnp.float32) - bsrc[:, cols].astype(jnp.float32)
        isrc[:, cols] = (g_ref[:, cols] * diff).astype(jnp.bfloat16)

    loop(0, GROUPS, innovation)
    pl.semaphore_wait(barrier, 64)

    row = c * 32 + m
    keep = row == 2 * m + c
    send_w = remote(w_ref, wtab, wsem.at[0], wsem.at[1], 2 * x + row % 2, row // 2)

    @pl.when(jnp.logical_not(keep))
    def _():
        send_w.start()

    @pl.when(keep)
    def _():
        pltpu.make_async_copy(w_ref, wtab, wsem.at[1]).start()

    def target(t):
        i = t // 2
        tz = 4 * c + (z + i // 4) % 4
        ty = (y + i % 4) % 4
        return tz * 4 + ty, t % 2

    def main(src, win, send, recv, t):
        tm, tc = target(t)
        k = 2 * (tm % 16) + tc
        copy = remote(
            src.at[:, pl.ds(mult(k * OWN, OWN), OWN)],
            win.at[pl.ds(mult(SHARE * m, SHARE), SHARE), pl.ds(RIM, OWN)],
            send.at[t],
            recv.at[m],
            2 * x + tc,
            tm,
        )
        return copy, jnp.logical_and(tm == m, tc == c)

    def send_main(src, win, send, recv):
        def body(t):
            copy, mine = main(src, win, send, recv, t)

            @pl.when(jnp.logical_not(mine))
            def _():
                copy.start()

            @pl.when(mine)
            def _():
                pltpu.make_async_copy(
                    src.at[:, pl.ds(mult(place * OWN, OWN), OWN)],
                    win.at[pl.ds(mult(SHARE * m, SHARE), SHARE), pl.ds(RIM, OWN)],
                    recv.at[m],
                ).start()

        return body

    def end_main(src, win, send, recv):
        def body(t):
            copy, mine = main(src, win, send, recv, t)

            @pl.when(jnp.logical_not(mine))
            def _():
                copy.wait_send()

        return body

    def cross(src, win, send, recv, t):
        up = t % 2
        tz = 4 * c + t // 2
        k = 2 * ((4 * tz + 3 * up) % 16) + up
        first = k * OWN + up * (OWN - RIM)
        step = 2 * up - 1
        there = x * 8 + tz + step + 32
        tx = (there // 8) % 4
        tm = 4 * (there % 8) + 3 * (1 - up)
        tc = 1 - up
        from_ = src.at[:, pl.ds(mult(first, RIM), RIM)]
        to = win.at[
            pl.ds(mult(SHARE * m, SHARE), SHARE), pl.ds(mult((1 - up) * (WIDE - RIM), RIM), RIM)
        ]
        copy = remote(from_, to, send.at[t], recv.at[m], 2 * tx + tc, tm)
        mine = jnp.logical_and(jnp.logical_and(tm == m, tc == c), tx == x)
        return copy, mine, from_, to

    def send_cross(src, win, send, recv):
        def body(t):
            copy, mine, from_, to = cross(src, win, send, recv, t)

            @pl.when(jnp.logical_not(mine))
            def _():
                copy.start()

            @pl.when(mine)
            def _():
                pltpu.make_async_copy(from_, to, recv.at[m]).start()

        return body

    def end_cross(src, win, send, recv):
        def body(t):
            copy, mine, _, _ = cross(src, win, send, recv, t)

            @pl.when(jnp.logical_not(mine))
            def _():
                copy.wait_send()

        return body

    def arrive(ref, sem):
        pltpu.make_async_copy(ref, ref, sem).wait()

    def wait_main(win, recv):
        def body(s):
            arrive(
                win.at[pl.ds(mult(SHARE * s, SHARE), SHARE), pl.ds(RIM, OWN)], recv.at[s]
            )

        loop(0, GROUPS, body)

    def rims(win, send, recv):
        right = remote(
            win.at[:, pl.ds(OWN, RIM)], win.at[:, pl.ds(0, RIM)], send.at[0], recv.at[0],
            2 * x + 1 - c, (m + c) % GROUPS,
        )
        left = remote(
            win.at[:, pl.ds(RIM, RIM)], win.at[:, pl.ds(WIDE - RIM, RIM)], send.at[1], recv.at[1],
            2 * x + 1 - c, (m + c + GROUPS - 1) % GROUPS,
        )
        return right, left

    def send_rims(win, send, recv):
        right, left = rims(win, send, recv)

        @pl.when(has_right)
        def _():
            right.start()

        @pl.when(has_left)
        def _():
            left.start()

    def end_rims(win, send, recv):
        right, left = rims(win, send, recv)

        @pl.when(has_right)
        def _():
            right.wait_send()

        @pl.when(has_left)
        def _():
            left.wait_send()

    def wait_rim(win, recv, crossing, side):
        near = has_right if side else has_left
        cols = pl.ds(side * (WIDE - RIM), RIM)

        @pl.when(near)
        def _():
            arrive(win.at[:, cols], recv.at[side])

        @pl.when(jnp.logical_not(near))
        def _():
            def body(s):
                arrive(
                    win.at[pl.ds(mult(SHARE * s, SHARE), SHARE), cols], crossing.at[s]
                )

            loop(0, GROUPS, body)

    loop(0, GROUPS, send_main(b_ref, bwin, bs, br))
    loop(0, 8, send_cross(b_ref, bwin, bcs, bcr))
    loop(0, GROUPS // 2, send_main(isrc, iwin, js, jr))

    arrive(wtab, wsem.at[1])
    pick = (
        lax.broadcasted_iota(jnp.int32, (128, SPAN), 1) // PC
        == lax.broadcasted_iota(jnp.int32, (128, SPAN), 0)
    ).astype(jnp.float32)

    def spread(i):
        wexp[i] = jnp.dot(
            wtab[i], pick, preferred_element_type=jnp.float32, precision=lax.Precision.HIGHEST
        )

    loop(0, BLOCKS, spread)

    wait_main(bwin, br)
    send_rims(bwin, hbs, hbr)
    loop(GROUPS // 2, GROUPS, send_main(isrc, iwin, js, jr))
    loop(0, 8, send_cross(isrc, iwin, jcs, jcr))

    def perturb(i):
        cols = pl.ds(mult(i * 256, 256), 256)
        state = bwin[:, cols].astype(jnp.float32)
        mean = jnp.sum(state, axis=0, keepdims=True) * (1.0 / MEMBERS)
        pwin[:, cols] = (state - mean).astype(jnp.bfloat16)

    def covariance(i):
        own = pwin[:, pl.ds(mult(RIM + i * ROWS, ROWS), ROWS)]
        for part in range(3):
            width = SPAN // 3
            near = pwin[:, pl.ds(mult(i * ROWS + part * width, 256), width)]
            full = lax.dot_general(
                own, near, (((0,), (0,)), ((), ())), preferred_element_type=jnp.float32
            )
            for g in range(BLOCK):
                weight = wexp[i, g : g + 1, part * width : (part + 1) * width]
                cov[i, g * PC : (g + 1) * PC, part * width : (part + 1) * width] = (
                    full[g * PC : (g + 1) * PC] * weight
                ).astype(jnp.bfloat16)

    loop(4, 16, perturb)
    loop(4, 8, covariance)
    wait_rim(bwin, hbr, bcr, 0)
    loop(0, 4, perturb)
    loop(0, 4, covariance)
    wait_rim(bwin, hbr, bcr, 1)
    loop(16, 20, perturb)
    loop(8, 12, covariance)

    wait_main(iwin, jr)
    send_rims(iwin, hjs, hjr)

    def increment(i):
        near = iwin[:, pl.ds(mult(i * ROWS, ROWS), SPAN)]
        result = lax.dot_general(
            near, cov[i], (((1,), (1,)), ((), ())), preferred_element_type=jnp.float32
        )
        obuf[:, pl.ds(mult(i * ROWS, ROWS), ROWS)] = result.astype(jnp.bfloat16)

    def result(q, t):
        tm = ((z + t // 4) % 8) * 4 + (y + t % 4) % 4
        from_ = obuf.at[pl.ds(mult(SHARE * tm, SHARE), SHARE), pl.ds(q * PART, PART)]
        to = o_ref.at[:, pl.ds(mult(place * OWN + q * PART, PART), PART)]
        copy = remote(
            from_, to, osend.at[q, t], orecv.at[q, place], 2 * x + half, tm
        )
        return copy, jnp.logical_and(tm == m, half == c), from_, to

    def send_result(q):
        def body(t):
            copy, mine, from_, to = result(q, t)

            @pl.when(jnp.logical_not(mine))
            def _():
                copy.start()

            @pl.when(mine)
            def _():
                pltpu.make_async_copy(from_, to, orecv.at[q, place]).start()

        loop(0, GROUPS, body)

    def end_result(q):
        def sent(t):
            copy, mine, _, _ = result(q, t)

            @pl.when(jnp.logical_not(mine))
            def _():
                copy.wait_send()

        def arrived(k):
            arrive(o_ref.at[:, pl.ds(mult(k * OWN + q * PART, PART), PART)], orecv.at[q, k])

        loop(0, GROUPS, sent)
        loop(0, GROUPS, arrived)

    loop(4, 8, increment)
    send_result(1)
    wait_rim(iwin, hjr, jcr, 0)
    loop(0, 4, increment)
    send_result(0)
    wait_rim(iwin, hjr, jcr, 1)
    loop(8, 12, increment)
    send_result(2)

    @pl.when(jnp.logical_not(keep))
    def _():
        send_w.wait_send()

    loop(0, GROUPS, end_main(b_ref, bwin, bs, br))
    loop(0, 8, end_cross(b_ref, bwin, bcs, bcr))
    loop(0, GROUPS, end_main(isrc, iwin, js, jr))
    loop(0, 8, end_cross(isrc, iwin, jcs, jcr))
    end_rims(bwin, hbs, hbr)
    end_rims(iwin, hjs, hjr)
    end_result(1)
    end_result(0)
    end_result(2)


def shards(states, measured, precision, counts, near_patches, tiers):
    observed = (jnp.arange(PC, dtype=jnp.int32)[None, :] < counts[:, None]).reshape(1, -1)
    gain = jnp.where(observed, precision[None, :], jnp.float32(0.0))
    patches = near_patches.shape[0]
    total = patches * lax.axis_size("dom") * lax.axis_size("mem")
    local = jnp.arange(patches, dtype=jnp.int32)[:, None]
    own = (lax.axis_index("dom") * lax.axis_size("mem") + lax.axis_index("mem")) * patches + local
    offset = (near_patches - own + total + total // 2) % total - total // 2
    slot = local % BLOCK + REACH + offset
    weight = gc_taper(tiers.astype(jnp.float32) / NCLASS) / (MEMBERS - 1)
    hit = slot[:, :, None] == jnp.arange(128, dtype=jnp.int32)[None, None, :]
    table = jnp.sum(jnp.where(hit, weight[:, :, None], 0.0), axis=1)
    table = jnp.pad(table.reshape(BLOCKS, BLOCK, 128), ((0, 0), (0, 8 - BLOCK), (0, 0)))
    any_spec = pl.BlockSpec(memory_space=pl.ANY)
    dma = pltpu.SemaphoreType.DMA
    bf16 = jnp.bfloat16
    return pl.pallas_call(
        kernel,
        name="increment",
        out_shape=jax.ShapeDtypeStruct(states.shape, bf16),
        in_specs=[
            any_spec,
            any_spec,
            pl.BlockSpec(memory_space=pltpu.VMEM),
            pl.BlockSpec(memory_space=pltpu.VMEM),
        ],
        out_specs=any_spec,
        scratch_shapes=[
            pltpu.VMEM(states.shape, bf16),
            pltpu.VMEM(states.shape, bf16),
            pltpu.VMEM((MEMBERS, WIDE), bf16),
            pltpu.VMEM((MEMBERS, WIDE), bf16),
            pltpu.VMEM((MEMBERS, WIDE), bf16),
            pltpu.VMEM((BLOCKS, ROWS, SPAN), bf16),
            pltpu.VMEM((MEMBERS, OWN), bf16),
            pltpu.VMEM((BLOCKS, 8, 128), jnp.float32),
            pltpu.VMEM((BLOCKS, 8, SPAN), jnp.float32),
            dma((2,)),
            dma((2,)),
            dma((GROUPS,)),
            dma((GROUPS,)),
            dma((8,)),
            dma((GROUPS,)),
            dma((GROUPS,)),
            dma((GROUPS,)),
            dma((8,)),
            dma((GROUPS,)),
            dma((2,)),
            dma((2,)),
            dma((2,)),
            dma((2,)),
            dma((3, GROUPS)),
            dma((3, GROUPS)),
        ],
        compiler_params=pltpu.CompilerParams(
            collective_id=0, has_side_effects=True, vmem_limit_bytes=58 * 1024 * 1024
        ),
    )(states, measured, gain, table)


def solution(mesh):
    in_specs = (
        P("mem", "dom"),
        P("mem", "dom"),
        P("dom"),
        P("dom"),
        P(("dom", "mem"), None),
        P(("dom", "mem"), None),
    )
    return jax.shard_map(
        shards, mesh=mesh, in_specs=in_specs, out_specs=P("mem", "dom"), check_vma=False
    )
```

time: 453 us -> 264 us (0.58)
  Pallas kernels: 0 us -> 254 us
  waiting for transfers between devices: 177 us -> 0 us
  local copies, waits for them, and re-layouts: 105 us -> 4.79 us
  blocking collectives: 82.7 us -> 0 us
  matrix products: 42.8 us -> 0 us
  starting transfers between devices: 18.9 us -> 0 us
  other arithmetic: 23.2 us -> 4.45 us
    pallas_call x0 -> x1, Pallas kernels: none -> 254 us  [shards(): pl.pallas_call(kernel, name='increment', out_shape=jax.ShapeDtypeStruct(s...]
    all_to_all x2 -> x0, waiting for transfers between devices: 132 us -> none  [the longest x1 66.9 us: shards(): lax.all_to_all(departure_residual, 'mem', split_axis=1, concat_axis=0, ti...]
    mul x12 -> x0, local copies, waits for them, and re-layouts: 86.3 us -> none  [update_block(): covariance.reshape(block_size, PC, window_patches, PC)]
    all_to_all x1 -> x0, blocking collectives: 82.7 us -> none  [shards(): lax.all_to_all(increment, 'mem', split_axis=0, concat_axis=1, tiled=True)]
    ppermute x2 -> x0, waiting for transfers between devices: 45.2 us -> none  [the longest x1 45.2 us: with_halo(): lax.ppermute(lax.slice_in_dim(block, block.shape[dim] - width, None, axis...]
    dot_general x6 -> x0, matrix products: 42.8 us -> none  [update_block(): lax.dot_general(window_innov, covariance, (((1,), (1,)), ((), ())), prefe...]
    all_to_all x2 -> x0, starting transfers between devices: 17.4 us -> none  [the longest x1 11 us: shards(): lax.all_to_all(background_trajectories, 'mem', split_axis=1, concat_axis=...]
    squeeze x1 -> x0, local copies, waits for them, and re-layouts: 8.6 us -> none  [shards(): disturbed_operator_image = padded[0]]
  transfers between devices with their start and end apart: 4 -> 0, of which waited for: 3 -> 0; matrix products, arithmetic and copies ran while one was open for 3% -> 0% of each run, Pallas kernels for 0% -> 0%
where the time goes in v1:
time: 264 us; the launch traced here: 263 us
  Pallas kernels  254 us (96%)
  local copies, waits for them, and re-layouts  4.79 us (2%)
  other arithmetic  4.45 us (2%)
    pallas_call x1, Pallas kernels, shards(): pl.pallas_call(kernel, name='increment', out_shape=jax.ShapeDtypeStruct(s...  254 us

profile of v1, /device:TPU:25, one launch (start us, length us, event | category | flops | bytes accessed | tf_op | source)
XLA Modules:
  0.0 263.2 jit_solution(3424131846355204947)
XLA Ops:
  0.0 0.7 fusion.10
  0.7 0.7 fusion.4
  1.4 0.1 copy.12
  1.5 0.1 copy.11
  1.6 0.3 select_reduce_fusion
  1.9 0.6 pad.4.w_ref
  2.5 1.0 iota_compare_fusion
  3.5 0.3 lt.32
  3.7 1.8 broadcast_select_fusion
  5.5 254.0 %increment.1 = bf16[16,98304]{1,0:T(8,128)(2,1)} custom-call(bf16[16,98304]{1,0:T(8,128)(2,1)} %b_ref.1, bf16[16,98304]{1,0:T(8,128)(2,1)} %j_ref.1, f32[1,98304]{1,0:T(1,128)} %bitcast.2, f32[12,8,128]{2,1,0:T(8,128)} %pad.4.w_ref), custom_call_target="tpu_custom_call" | custom-call | tf_op jit(solution)/shard_map/increment/pallas_call | solution.py:431
  259.5 3.8 %copy.14 = bf16[16,98304]{1,0:T(8,128)(2,1)} copy(bf16[16,98304]{1,0:T(8,128)(2,1)} %increment.1) | data formatting | bytes 6291456
  (1 shorter events, 0.0 us)

commit v2 on v1

v2 whole, which is shorter than its diff:
```python
import jax
import jax.numpy as jnp
from jax import lax
from jax.experimental import pallas as pl
from jax.experimental.pallas import tpu as pltpu
from jax.sharding import PartitionSpec as P

PC = 64
REACH = 16
NCLASS = 8
MEMBERS = 512
GROUPS = 32
SHARE = MEMBERS // GROUPS
OWN = 3072
RIM = REACH * PC
WIDE = OWN + 2 * RIM
BLOCK = 4
ROWS = BLOCK * PC
SPAN = ROWS + 2 * RIM
BLOCKS = OWN // ROWS
TEAM = MEMBERS // 4


def gc_taper(r):
    return 1.0 - 5.0 / 3.0 * r**2 + 0.625 * r**3 + 0.5 * r**4 - 0.25 * r**5


def mult(value, by):
    return pl.multiple_of(value, by)


def kernel(
    b_ref,
    j_ref,
    g_ref,
    n_ref,
    a_ref,
    t_ref,
    o_ref,
    bsrc,
    isrc,
    bwin,
    iwin,
    pwin,
    cov,
    obuf,
    nexp,
    atab,
    ttab,
    wexp,
    lsem,
    wsem,
    bs,
    br,
    bcs,
    bcr,
    js,
    jr,
    jcs,
    jcr,
    hbs,
    hbr,
    hjs,
    hjr,
    osend,
    orecv,
):
    d = lax.axis_index("dom")
    m = lax.axis_index("mem")
    x, c = d // 2, d % 2
    z, y = m // 4, m % 4
    turn = 1 + 2 * (z % 2)
    seat = (z % 4) * 8 + (z // 4) * 4 + y
    half = m // 16
    place = 2 * (m % 16) + c
    has_left = jnp.logical_or(c == 1, y > 0)
    has_right = jnp.logical_or(c == 0, y < 3)

    def loop(start, stop, body):
        def step(i, carry):
            body(i)
            return carry

        lax.fori_loop(start, stop, step, 0)

    def remote(src, dst, send, recv, dom, mem):
        return pltpu.make_async_remote_copy(
            src_ref=src,
            dst_ref=dst,
            send_sem=send,
            recv_sem=recv,
            device_id={"dom": dom, "mem": mem},
            device_id_type=pl.DeviceIdType.MESH,
        )

    load_b = pltpu.make_async_copy(b_ref, bsrc, lsem.at[0])
    load_j = pltpu.make_async_copy(j_ref, isrc, lsem.at[1])
    load_b.start()
    load_j.start()
    barrier = pltpu.get_barrier_semaphore()

    def greet(t):
        other = (c * 32 + m + t) % 64
        pl.semaphore_signal(
            barrier, inc=1, device_id={"dom": 2 * x + other // 32, "mem": other % 32}
        )

    loop(1, 64, greet)

    @pl.when(jnp.logical_and(c == 0, m == 0))
    def _():
        def greet_lower(t):
            pl.semaphore_signal(
                barrier, inc=1, device_id={"dom": 2 * ((x + 3) % 4) + 1, "mem": t}
            )

        loop(0, GROUPS, greet_lower)

    @pl.when(jnp.logical_and(c == 1, m == GROUPS - 1))
    def _():
        def greet_upper(t):
            pl.semaphore_signal(barrier, inc=1, device_id={"dom": 2 * ((x + 1) % 4), "mem": t})

        loop(0, GROUPS, greet_upper)

    pl.semaphore_wait(barrier, 64)

    row = c * 32 + m
    keep = row == 2 * m + c
    send_a = remote(a_ref, atab, wsem.at[0], wsem.at[1], 2 * x + row % 2, row // 2)
    send_t = remote(t_ref, ttab, wsem.at[2], wsem.at[3], 2 * x + row % 2, row // 2)

    def send_lists():
        @pl.when(jnp.logical_not(keep))
        def _():
            send_a.start()
            send_t.start()

        @pl.when(keep)
        def _():
            pltpu.make_async_copy(a_ref, atab, wsem.at[1]).start()
            pltpu.make_async_copy(t_ref, ttab, wsem.at[3]).start()

    def target(t):
        tz = 4 * c + (z + turn * (t // 8)) % 4
        ty = (y + (t // 2) % 4) % 4
        return tz * 4 + ty, t % 2

    def main(src, win, send, recv, t):
        tm, tc = target(t)
        k = 2 * (tm % 16) + tc
        copy = remote(
            src.at[:, pl.ds(mult(k * OWN, OWN), OWN)],
            win.at[pl.ds(mult(SHARE * seat, SHARE), SHARE), pl.ds(RIM, OWN)],
            send.at[t],
            recv.at[seat],
            2 * x + tc,
            tm,
        )
        return copy, jnp.logical_and(tm == m, tc == c)

    def send_main(src, win, send, recv):
        def body(t):
            copy, mine = main(src, win, send, recv, t)

            @pl.when(jnp.logical_not(mine))
            def _():
                copy.start()

            @pl.when(mine)
            def _():
                pltpu.make_async_copy(
                    src.at[:, pl.ds(mult(place * OWN, OWN), OWN)],
                    win.at[pl.ds(mult(SHARE * seat, SHARE), SHARE), pl.ds(RIM, OWN)],
                    recv.at[seat],
                ).start()

        return body

    def end_main(src, win, send, recv):
        def body(t):
            copy, mine = main(src, win, send, recv, t)

            @pl.when(jnp.logical_not(mine))
            def _():
                copy.wait_send()

        return body

    def cross(src, win, send, recv, t):
        up = t % 2
        tz = 4 * c + (z + turn * (t // 2) + 1 + 2 * up) % 4
        k = 2 * ((4 * tz + 3 * up) % 16) + up
        first = k * OWN + up * (OWN - RIM)
        step = 2 * up - 1
        there = x * 8 + tz + step + 32
        tx = (there // 8) % 4
        tm = 4 * (there % 8) + 3 * (1 - up)
        tc = 1 - up
        from_ = src.at[:, pl.ds(mult(first, RIM), RIM)]
        to = win.at[
            pl.ds(mult(SHARE * seat, SHARE), SHARE), pl.ds(mult((1 - up) * (WIDE - RIM), RIM), RIM)
        ]
        copy = remote(from_, to, send.at[t], recv.at[seat], 2 * tx + tc, tm)
        mine = jnp.logical_and(jnp.logical_and(tm == m, tc == c), tx == x)
        return copy, mine, from_, to

    def send_cross(src, win, send, recv):
        def body(t):
            copy, mine, from_, to = cross(src, win, send, recv, t)

            @pl.when(jnp.logical_not(mine))
            def _():
                copy.start()

            @pl.when(mine)
            def _():
                pltpu.make_async_copy(from_, to, recv.at[seat]).start()

        return body

    def end_cross(src, win, send, recv):
        def body(t):
            copy, mine, _, _ = cross(src, win, send, recv, t)

            @pl.when(jnp.logical_not(mine))
            def _():
                copy.wait_send()

        return body

    def arrive(ref, sem):
        pltpu.make_async_copy(ref, ref, sem).wait()

    def wait_main(win, recv, team):
        def body(s):
            arrive(
                win.at[pl.ds(mult(SHARE * s, SHARE), SHARE), pl.ds(RIM, OWN)], recv.at[s]
            )

        loop(team * 8, team * 8 + 8, body)

    def rims(win, send, recv, team):
        rows = pl.ds(mult(team * TEAM, TEAM), TEAM)
        right = remote(
            win.at[rows, pl.ds(OWN, RIM)], win.at[rows, pl.ds(0, RIM)],
            send.at[0, team], recv.at[0, team], 2 * x + 1 - c, (m + c) % GROUPS,
        )
        left = remote(
            win.at[rows, pl.ds(RIM, RIM)], win.at[rows, pl.ds(WIDE - RIM, RIM)],
            send.at[1, team], recv.at[1, team], 2 * x + 1 - c, (m + c + GROUPS - 1) % GROUPS,
        )
        return right, left

    def send_rims(win, send, recv, team):
        right, left = rims(win, send, recv, team)

        @pl.when(has_right)
        def _():
            right.start()

        @pl.when(has_left)
        def _():
            left.start()

    def end_rims(win, send, recv, team):
        right, left = rims(win, send, recv, team)

        @pl.when(has_right)
        def _():
            right.wait_send()

        @pl.when(has_left)
        def _():
            left.wait_send()

    def wait_rim(win, recv, crossing, side, team):
        near = has_right if side else has_left
        cols = pl.ds(side * (WIDE - RIM), RIM)

        @pl.when(near)
        def _():
            arrive(win.at[pl.ds(mult(team * TEAM, TEAM), TEAM), cols], recv.at[side, team])

        @pl.when(jnp.logical_not(near))
        def _():
            def body(s):
                arrive(
                    win.at[pl.ds(mult(SHARE * s, SHARE), SHARE), cols], crossing.at[s]
                )

            loop(team * 8, team * 8 + 8, body)

    def members_out(src, win, send, recv, csend, crecv, phase):
        loop(phase * 8, phase * 8 + 8, send_main(src, win, send, recv))
        loop(phase * 2, phase * 2 + 2, send_cross(src, win, csend, crecv))

    def states_out(phase):
        members_out(b_ref, bwin, bs, br, bcs, bcr, phase)

    def innovations_out(phase):
        members_out(isrc, iwin, js, jr, jcs, jcr, phase)

    def team_of(phase):
        return (z + turn * phase) % 4

    loop(0, 4, states_out)
    send_lists()

    pick_patch = (
        lax.broadcasted_iota(jnp.int32, (48, OWN), 1) // PC
        == lax.broadcasted_iota(jnp.int32, (48, OWN), 0)
    ).astype(jnp.bfloat16)
    counts = n_ref[...].astype(jnp.float32).astype(jnp.bfloat16)
    nexp[...] = jnp.dot(counts, pick_patch, preferred_element_type=jnp.float32)
    cell = (lax.broadcasted_iota(jnp.int32, (1, OWN), 1) % PC).astype(jnp.float32)
    load_b.wait()
    load_j.wait()

    def innovation(k):
        cols = pl.ds(mult(k * OWN, OWN), OWN)
        gain = jnp.where(cell < nexp[pl.ds(k, 1), :], g_ref[:, cols], 0.0)
        diff = isrc[:, cols].astype(jnp.float32) - bsrc[:, cols].astype(jnp.float32)
        isrc[:, cols] = (gain * diff).astype(jnp.bfloat16)

    loop(0, GROUPS, innovation)
    loop(0, 2, innovations_out)

    arrive(atab, wsem.at[1])
    arrive(ttab, wsem.at[3])
    local = lax.broadcasted_iota(jnp.int32, (48, 16), 0)
    offset = atab[...] - ((64 * x + 2 * m + c) * 48 + local)
    total = 256 * 48
    offset = jnp.where(offset > REACH, offset - total, offset)
    offset = jnp.where(offset < -REACH, offset + total, offset)
    slot = local % BLOCK + REACH + offset
    weight = gc_taper(ttab[...].astype(jnp.float32) / NCLASS) / (MEMBERS - 1)
    lane = lax.broadcasted_iota(jnp.int32, (48, 128), 1)
    table = jnp.zeros((48, 128), jnp.float32)
    for j in range(16):
        table = table + jnp.where(lane == slot[:, j : j + 1], weight[:, j : j + 1], 0.0)
    pick = (
        lax.broadcasted_iota(jnp.int32, (128, SPAN), 1) // PC
        == lax.broadcasted_iota(jnp.int32, (128, SPAN), 0)
    ).astype(jnp.float32)
    wide = jnp.dot(
        table, pick, preferred_element_type=jnp.float32, precision=lax.Precision.HIGHEST
    )
    for i in range(BLOCKS):
        wexp[i, 0:BLOCK, :] = wide[i * BLOCK : (i + 1) * BLOCK]

    loop(0, 4, lambda team: wait_main(bwin, br, team))
    loop(0, 4, lambda team: send_rims(bwin, hbs, hbr, team))
    innovations_out(2)

    def perturb(i):
        cols = pl.ds(mult(i * 256, 256), 256)
        state = bwin[:, cols].astype(jnp.float32)
        mean = jnp.sum(state, axis=0, keepdims=True) * (1.0 / MEMBERS)
        pwin[:, cols] = (state - mean).astype(jnp.bfloat16)

    def covariance(i):
        own = pwin[:, pl.ds(mult(RIM + i * ROWS, ROWS), ROWS)]
        for part in range(3):
            width = SPAN // 3
            near = pwin[:, pl.ds(mult(i * ROWS + part * width, 256), width)]
            full = lax.dot_general(
                own, near, (((0,), (0,)), ((), ())), preferred_element_type=jnp.float32
            )
            for g in range(BLOCK):
                weight = wexp[i, g : g + 1, part * width : (part + 1) * width]
                cov[i, g * PC : (g + 1) * PC, part * width : (part + 1) * width] = (
                    full[g * PC : (g + 1) * PC] * weight
                ).astype(jnp.bfloat16)

    def innovations_in(phase):
        team = team_of(phase)
        wait_main(iwin, jr, team)
        send_rims(iwin, hjs, hjr, team)

    def result(team, t):
        s = (y + t) % 4
        tm = (team + 4 * ((z // 4 + t // 4) % 2)) * 4 + s
        tseat = team * 8 + ((z // 4 + t // 4) % 2) * 4 + s
        from_ = obuf.at[pl.ds(mult(SHARE * tseat, SHARE), SHARE), :]
        to = o_ref.at[:, pl.ds(mult(place * OWN, OWN), OWN)]
        copy = remote(from_, to, osend.at[tseat], orecv.at[place], 2 * x + half, tm)
        return copy, jnp.logical_and(tm == m, half == c), from_, to

    def send_result(team):
        def body(t):
            copy, mine, from_, to = result(team, t)

            @pl.when(jnp.logical_not(mine))
            def _():
                copy.start()

            @pl.when(mine)
            def _():
                pltpu.make_async_copy(from_, to, orecv.at[place]).start()

        loop(0, 8, body)

    def end_result(team):
        def sent(t):
            copy, mine, _, _ = result(team, t)

            @pl.when(jnp.logical_not(mine))
            def _():
                copy.wait_send()

        loop(0, 8, sent)

    def increments_out(phase):
        team = team_of(phase)
        rows = pl.ds(mult(team * TEAM, TEAM), TEAM)
        wait_rim(iwin, hjr, jcr, 0, team)
        wait_rim(iwin, hjr, jcr, 1, team)

        def increment(i):
            near = iwin[rows, pl.ds(mult(i * ROWS, ROWS), SPAN)]
            made = lax.dot_general(
                near, cov[i], (((1,), (1,)), ((), ())), preferred_element_type=jnp.float32
            )
            obuf[rows, pl.ds(mult(i * ROWS, ROWS), ROWS)] = made.astype(jnp.bfloat16)

        loop(0, BLOCKS, increment)
        send_result(team)

    loop(4, 16, perturb)
    loop(4, 8, covariance)
    innovations_in(0)
    innovations_out(3)
    loop(0, 4, lambda team: wait_rim(bwin, hbr, bcr, 0, team))
    loop(0, 4, perturb)
    loop(0, 4, covariance)
    loop(0, 4, lambda team: wait_rim(bwin, hbr, bcr, 1, team))
    loop(16, 20, perturb)
    loop(8, 12, covariance)

    def stage(phase):
        innovations_in(phase + 1)
        increments_out(phase)

    loop(0, 3, stage)
    increments_out(3)

    @pl.when(jnp.logical_not(keep))
    def _():
        send_a.wait_send()
        send_t.wait_send()

    loop(0, GROUPS, end_main(b_ref, bwin, bs, br))
    loop(0, 8, end_cross(b_ref, bwin, bcs, bcr))
    loop(0, GROUPS, end_main(isrc, iwin, js, jr))
    loop(0, 8, end_cross(isrc, iwin, jcs, jcr))
    loop(0, 4, lambda team: end_rims(bwin, hbs, hbr, team))
    loop(0, 4, lambda team: end_rims(iwin, hjs, hjr, team))
    loop(0, 4, end_result)
    loop(
        0,
        GROUPS,
        lambda k: arrive(o_ref.at[:, pl.ds(mult(k * OWN, OWN), OWN)], orecv.at[k]),
    )


def shards(states, measured, precision, counts, near_patches, tiers):
    any_spec = pl.BlockSpec(memory_space=pl.ANY)
    dma = pltpu.SemaphoreType.DMA
    bf16 = jnp.bfloat16
    return pl.pallas_call(
        kernel,
        name="increment",
        out_shape=jax.ShapeDtypeStruct(states.shape, bf16),
        in_specs=[
            any_spec,
            any_spec,
            pl.BlockSpec(memory_space=pltpu.VMEM),
            pl.BlockSpec(memory_space=pltpu.VMEM),
            any_spec,
            any_spec,
        ],
        out_specs=any_spec,
        scratch_shapes=[
            pltpu.VMEM(states.shape, bf16),
            pltpu.VMEM(states.shape, bf16),
            pltpu.VMEM((MEMBERS, WIDE), bf16),
            pltpu.VMEM((MEMBERS, WIDE), bf16),
            pltpu.VMEM((MEMBERS, WIDE), bf16),
            pltpu.VMEM((BLOCKS, ROWS, SPAN), bf16),
            pltpu.VMEM((MEMBERS, OWN), bf16),
            pltpu.VMEM((GROUPS, OWN), jnp.float32),
            pltpu.VMEM(near_patches.shape, jnp.int32),
            pltpu.VMEM(near_patches.shape, jnp.int32),
            pltpu.VMEM((BLOCKS, 8, SPAN), jnp.float32),
            dma((2,)),
            dma((4,)),
            dma((GROUPS,)),
            dma((GROUPS,)),
            dma((8,)),
            dma((GROUPS,)),
            dma((GROUPS,)),
            dma((GROUPS,)),
            dma((8,)),
            dma((GROUPS,)),
            dma((2, 4)),
            dma((2, 4)),
            dma((2, 4)),
            dma((2, 4)),
            dma((GROUPS,)),
            dma((GROUPS,)),
        ],
        compiler_params=pltpu.CompilerParams(
            collective_id=0, has_side_effects=True, vmem_limit_bytes=58 * 1024 * 1024
        ),
    )(
        states,
        measured,
        precision.reshape(1, -1),
        counts.reshape(GROUPS, -1),
        near_patches,
        tiers,
    )


def solution(mesh):
    in_specs = (
        P("mem", "dom"),
        P("mem", "dom"),
        P("dom"),
        P("dom"),
        P(("dom", "mem"), None),
        P(("dom", "mem"), None),
    )
    return jax.shard_map(
        shards, mesh=mesh, in_specs=in_specs, out_specs=P("mem", "dom"), check_vma=False
    )
```

time: 264 us -> 247 us (0.936)
  the two profiles are of different devices: /device:TPU:25 before, /device:TPU:66 now
where the time goes in v2:
time: 247 us
  Pallas kernels  239 us (97%)
  local copies, waits for them, and re-layouts  7.88 us (3%)
    pallas_call x1, Pallas kernels, shards(): pl.pallas_call(kernel, name='increment', out_shape=jax.ShapeDtypeStruct(s...  239 us
    unnamed x3, local copies, waits for them, and re-layouts  6.51 us

profile of v2, /device:TPU:66, one launch (start us, length us, event | category | flops | bytes accessed | tf_op | source)
XLA Modules:
  0.0 247.2 jit_solution(18267984572406323647)
XLA Ops:
  0.0 1.4 reshape.7.n_ref
  1.4 1.4 copy.7.a_ref
  2.8 1.4 copy.8.t_ref
  4.1 239.3 %increment.1 = bf16[16,98304]{1,0:T(8,128)(2,1)} custom-call(bf16[16,98304]{1,0:T(8,128)(2,1)} %b_ref.1, bf16[16,98304]{1,0:T(8,128)(2,1)} %j_ref.1, f32[1,98304]{1,0:T(1,128)} %bitcast.1, s32[32,48]{1,0:T(8,128)} %reshape.7.n_ref, s32[48,16]{1,0:T(8,128)} %copy.7.a_ref, s32[48,16]{1,0:T(8,128)} %copy.8.t_ref), custom_call_target="tpu_custom_call" | custom-call | tf_op jit(solution)/shard_map/increment/pallas_call | solution.py:471
  243.4 3.8 %copy.10 = bf16[16,98304]{1,0:T(8,128)(2,1)} copy(bf16[16,98304]{1,0:T(8,128)(2,1)} %increment.1) | data formatting | bytes 6291456
